TPU v7x, 32 devices: a whole 2x2x4 slice. The times are simulated.
32 devices in a mesh: dp: 4 (over y, core), expert: 2 (over x), tensor: 4 (over z).
Axes of the slice: x: 2, y: 2, z: 4, core: 2. Of those that a mesh axis runs over, the one named last changes fastest.
Arguments:
- inputs: bfloat16 [1576, 768], P(('dp', 'expert')), may hold values from -6 to 6
- first_gain: float32 [768], replicated, may hold values from 0.5 to 1.5
- first_bias: float32 [768], replicated, may hold values from -2 to 2
- attention_in: bfloat16 [3, 768, 768], P(None, None, 'tensor')
- attention_out: bfloat16 [768, 768], P('tensor'), may hold values from -0.875 to 0.875
- second_gain: float32 [768], replicated, may hold values from 0.5 to 1.5
- second_bias: float32 [768], replicated, may hold values from -2 to 2
- router_weight: float32 [768, 4], replicated
- expert_in: bfloat16 [4, 768, 3072], P('expert', None, 'tensor'), may hold values from -0.21875 to 0.21875
- expert_out: bfloat16 [4, 3072, 768], P('expert', 'tensor'), may hold values from -1.75 to 1.75
- expert_ids: int32 [1576, 2], P(('dp', 'expert')), may hold values from 0 to 3, as said below
- slot_index: int32 [1576, 2], P(('dp', 'expert')), may hold values from 0 to 98, as said below
- cotangent: bfloat16 [1576, 768], P(('dp', 'expert')), may hold values from -6 to 6
Outputs:
- layer_out: float32 [1576, 768], P(('dp', 'expert'))
- input_grad: float32 [1576, 768], P(('dp', 'expert'))
- first_gain_grad: float32 [768], P(('dp', 'expert'))
- first_bias_grad: float32 [768], P(('dp', 'expert'))
- attention_in_grad: float32 [3, 768, 768], P(None, ('dp', 'expert'), 'tensor')
- attention_out_grad: float32 [768, 768], P('tensor', ('dp', 'expert'))
- second_gain_grad: float32 [768], P(('dp', 'expert'))
- second_bias_grad: float32 [768], P(('dp', 'expert'))
- router_grad: float32 [768, 4], P(('dp', 'expert'))
- expert_in_grad: float32 [4, 768, 3072], P('expert', 'dp', 'tensor')
- expert_out_grad: float32 [4, 3072, 768], P('expert', 'tensor', 'dp')
Inputs may be any that keep to these rules, and one draw needn't show every extreme that they name: `expert_ids`: the two experts of a token differ. `slot_index`: among the 197 tokens of one index of dp and expert, the choices naming one expert hold slots 0, 1, 2 and so on, all first choices before all second choices, rows in order within each; a choice ranked 98 or later holds 98 and is dropped. Some expert fills all 98 slots from every index of dp and expert.
All inputs are finite; a program needn't handle non-finite values.
Results may differ from a plain program's by a relative error of at most 0.02.
Values may be sent and summed in bfloat16 or wider, within the bound.
A program may use at most 128 MiB of HBM per device.

v0:
```python
import math
import jax
import jax.numpy as jnp
from jax import lax
from jax.sharding import PartitionSpec as P

HEAD_DIM = 64
SEQ = 197
EPS = 1e-06
GELU_C = math.sqrt(2.0 / math.pi)


def cut_along(shard, dim, devices):
    shape = shard.shape
    tiles = shard.reshape(*shape[:dim], devices, shape[dim] // devices, *shape[dim + 1 :])
    return jnp.moveaxis(tiles, dim, 0)


def sent_and_summed(shard, axis, dim):
    devices = lax.axis_size(axis)
    tiles = lax.all_to_all(cut_along(shard, dim, devices), axis, 0, 0, tiled=True)
    return jnp.sum(tiles.astype(jnp.float32), axis=0)


def sent_together(arrays, axis, dim, along):
    widths = [math.prod(a.shape[along:]) for a in arrays]
    both = jnp.concatenate(
        [a.reshape(*a.shape[:along], w) for a, w in zip(arrays, widths)], axis=along
    )
    out = sent_and_summed(both, axis, dim)
    tiles = jnp.split(out, [sum(widths[:k]) for k in range(1, len(widths))], axis=along)
    return tuple((b.reshape(*out.shape[:along], *a.shape[along:]) for a, b in zip(arrays, tiles)))


def normalize(values):
    centre = jnp.mean(values, axis=-1, keepdims=True)
    centred = values - centre
    spread = jnp.mean(centred * centred, axis=-1, keepdims=True)
    scale = lax.rsqrt(spread + EPS)
    return (centred * scale, scale)


def norm_back(grad_out, normed, scale, gain):
    scaled = grad_out * gain
    first_mean = jnp.mean(scaled, axis=-1, keepdims=True)
    second_mean = jnp.mean(scaled * normed, axis=-1, keepdims=True)
    return scale * (scaled - first_mean - normed * second_mean)


def gelu_parts(pre):
    inner = GELU_C * (pre + 0.044715 * pre * pre * pre)
    tangent = jnp.tanh(inner)
    value = 0.5 * pre * (1.0 + tangent)
    slope = 0.5 * (1.0 + tangent) + 0.5 * pre * (1.0 - tangent * tangent) * GELU_C * (
        1.0 + 3.0 * 0.044715 * pre * pre
    )
    return (value, slope)


def per_device(
    inputs,
    first_gain,
    first_bias,
    attention_in,
    attention_out,
    second_gain,
    second_bias,
    router_weight,
    expert_in,
    expert_out,
    expert_ids,
    slot_index,
    cotangent,
):
    tokens_here = inputs.shape[0]
    model_width = inputs.shape[1]
    images = tokens_here // SEQ
    local_width = attention_in.shape[2]
    local_heads = local_width // HEAD_DIM
    owners = lax.axis_size("expert")
    experts_here = expert_in.shape[0]
    experts_all = experts_here * owners
    capacity = (2 * tokens_here - 1) // experts_all
    scaling = HEAD_DIM ** (-0.5)

    def split_heads(matrix):
        return matrix.reshape(images, SEQ, local_heads, HEAD_DIM)

    x_full = inputs.astype(jnp.float32)
    normed1, scale1 = normalize(x_full)
    first = (normed1 * first_gain + first_bias).astype(jnp.bfloat16)
    project = [
        jnp.dot(first, attention_in[which], preferred_element_type=jnp.float32).astype(jnp.bfloat16)
        for which in range(3)
    ]
    query_h, keys_h, values_h = [split_heads(part) for part in project]
    scores = (
        jnp.einsum("iqhd,ikhd->ihqk", query_h, keys_h, preferred_element_type=jnp.float32) * scaling
    )
    peak = jnp.max(scores, axis=-1, keepdims=True)
    logsum = peak[..., 0] + jnp.log(jnp.sum(jnp.exp(scores - peak), axis=-1))
    weights = jnp.exp(scores - logsum[..., None]).astype(jnp.bfloat16)
    context_h = jnp.einsum(
        "ihqk,ikhd->iqhd", weights, values_h, preferred_element_type=jnp.float32
    ).astype(jnp.bfloat16)
    context = context_h.reshape(tokens_here, local_width)
    partial_attn = jnp.dot(context, attention_out, preferred_element_type=jnp.float32)
    attended = lax.psum(partial_attn, "tensor")
    resid = x_full + attended
    normed2, scale2 = normalize(resid)
    second = (normed2 * second_gain + second_bias).astype(jnp.bfloat16)
    logits = jnp.dot(second.astype(jnp.float32), router_weight, precision=lax.Precision.HIGHEST)
    route = jax.nn.softmax(logits, axis=-1)
    valid = (slot_index < capacity).astype(jnp.float32)
    choose = (expert_ids[:, :, None] == jnp.arange(experts_all, dtype=jnp.int32)).astype(
        jnp.float32
    )
    gate = jnp.sum(route[:, None, :] * choose, axis=-1) * valid
    target = jnp.where(slot_index < capacity, expert_ids * capacity + slot_index, -1)
    chosen = (target[:, :, None] == jnp.arange(experts_all * capacity, dtype=jnp.int32)).astype(
        jnp.bfloat16
    )
    placing = jnp.sum(chosen, axis=1)
    sendbuf = jnp.einsum("rq,rd->qd", placing, second, preferred_element_type=jnp.float32).astype(
        jnp.bfloat16
    )
    sendbuf = sendbuf.reshape(owners, experts_here, capacity, model_width)
    received = lax.all_to_all(sendbuf, "expert", split_axis=0, concat_axis=0, tiled=True)
    pre = jnp.einsum("skcd,kdf->skcf", received, expert_in, preferred_element_type=jnp.float32)
    value, slope = gelu_parts(pre)
    hidden = value.astype(jnp.bfloat16)
    partial_value = jnp.einsum(
        "skcf,kfd->skcd", hidden, expert_out, preferred_element_type=jnp.float32
    )
    summed = lax.psum(partial_value, "tensor")
    returned = lax.all_to_all(
        summed.astype(jnp.bfloat16), "expert", split_axis=0, concat_axis=0, tiled=True
    )
    outcome = (returned, received, hidden, slope)
    returned = outcome[0]
    received = outcome[1]
    outputs_flat = returned.reshape(experts_all * capacity, model_width)
    picked = jnp.einsum("rjq,qd->rjd", chosen, outputs_flat, preferred_element_type=jnp.float32)
    layer_out = resid + jnp.sum(gate[..., None] * picked, axis=1)
    grad_out = cotangent.astype(jnp.float32)
    gate_grad = jnp.sum(grad_out[:, None, :] * picked, axis=-1) * valid
    slot_gate = jnp.einsum(
        "rjq,rj->q", chosen.astype(jnp.float32), gate, precision=lax.Precision.HIGHEST
    )
    slotted = jnp.einsum("rq,rd->qd", placing, cotangent, preferred_element_type=jnp.float32)
    grad_send = (
        (slot_gate[:, None] * slotted)
        .astype(jnp.bfloat16)
        .reshape(owners, experts_here, capacity, model_width)
    )
    grad_recv = lax.all_to_all(grad_send, "expert", split_axis=0, concat_axis=0, tiled=True)
    hidden = outcome[2]
    slope = outcome[3]
    hidden_grad = jnp.einsum(
        "skcd,kfd->skcf", grad_recv, expert_out, preferred_element_type=jnp.float32
    )
    pre_grad = (hidden_grad * slope).astype(jnp.bfloat16)
    local_out_grad = jnp.einsum(
        "skcf,skcd->kfd", hidden, grad_recv, preferred_element_type=jnp.float32
    )
    local_in_grad = jnp.einsum(
        "skcd,skcf->kdf", received, pre_grad, preferred_element_type=jnp.float32
    )
    partial_back = jnp.einsum(
        "skcf,kdf->skcd", pre_grad, expert_in, preferred_element_type=jnp.float32
    )
    back_sum = lax.psum(partial_back.astype(jnp.bfloat16), "tensor")
    back_home = lax.all_to_all(back_sum, "expert", split_axis=0, concat_axis=0, tiled=True)
    back_rows = jnp.einsum(
        "rjq,qd->rd",
        chosen,
        back_home.reshape(experts_all * capacity, model_width),
        preferred_element_type=jnp.float32,
    )
    expert_in_grad, expert_out_grad = (
        lax.psum_scatter(
            local_in_grad.astype(jnp.bfloat16), "dp", scatter_dimension=1, tiled=True
        ).astype(jnp.float32),
        lax.psum_scatter(
            local_out_grad.astype(jnp.bfloat16), "dp", scatter_dimension=2, tiled=True
        ).astype(jnp.float32),
    )
    route_grad = jnp.sum(gate_grad[:, :, None] * choose, axis=1)
    logit_grad = route * (route_grad - jnp.sum(route * route_grad, axis=-1, keepdims=True))
    local_router = jnp.dot(
        second.astype(jnp.float32).T, logit_grad, precision=lax.Precision.HIGHEST
    )
    second_grad = back_rows + jnp.dot(logit_grad, router_weight.T, precision=lax.Precision.HIGHEST)
    local_second_gain = jnp.sum(second_grad * normed2, axis=0)
    local_second_bias = jnp.sum(second_grad, axis=0)
    resid_grad = grad_out + norm_back(second_grad, normed2, scale2, second_gain)
    resid_low = resid_grad.astype(jnp.bfloat16)
    local_attn_out = jnp.einsum("rh,rd->hd", context, resid_low, preferred_element_type=jnp.float32)
    context_grad = jnp.einsum(
        "rd,hd->rh", resid_low, attention_out, preferred_element_type=jnp.float32
    ).astype(jnp.bfloat16)
    context_g = split_heads(context_grad)
    probs = jnp.exp(scores - logsum[..., None])
    values_grad = jnp.einsum(
        "ihqk,iqhd->ikhd", weights, context_g, preferred_element_type=jnp.float32
    ).astype(jnp.bfloat16)
    probs_grad = jnp.einsum(
        "iqhd,ikhd->ihqk", context_g, values_h, preferred_element_type=jnp.float32
    )
    delta = jnp.transpose(
        jnp.sum(context_g.astype(jnp.float32) * context_h.astype(jnp.float32), axis=-1), (0, 2, 1)
    )
    score_grad = (probs * (probs_grad - delta[..., None]) * scaling).astype(jnp.bfloat16)
    query_grad = jnp.einsum(
        "ihqk,ikhd->iqhd", score_grad, keys_h, preferred_element_type=jnp.float32
    ).astype(jnp.bfloat16)
    keys_grad = jnp.einsum(
        "ihqk,iqhd->ikhd", score_grad, query_h, preferred_element_type=jnp.float32
    ).astype(jnp.bfloat16)
    grads_flat = [
        part.reshape(tokens_here, local_width) for part in (query_grad, keys_grad, values_grad)
    ]
    local_attn_in = jnp.stack(
        [
            jnp.einsum("rd,rh->dh", first, part, preferred_element_type=jnp.float32)
            for part in grads_flat
        ]
    )
    partial_first = jnp.einsum(
        "rh,dh->rd", grads_flat[0], attention_in[0], preferred_element_type=jnp.float32
    )
    partial_first = partial_first + jnp.einsum(
        "rh,dh->rd", grads_flat[1], attention_in[1], preferred_element_type=jnp.float32
    )
    partial_first = partial_first + jnp.einsum(
        "rh,dh->rd", grads_flat[2], attention_in[2], preferred_element_type=jnp.float32
    )
    first_grad = lax.psum(partial_first.astype(jnp.bfloat16), "tensor").astype(jnp.float32)
    local_first_gain = jnp.sum(first_grad * normed1, axis=0)
    local_first_bias = jnp.sum(first_grad, axis=0)
    input_grad = resid_grad + norm_back(first_grad, normed1, scale1, first_gain)
    summed_shared = (
        sent_and_summed(local_attn_in.astype(jnp.bfloat16), ("dp", "expert"), 1),
        sent_and_summed(local_attn_out.astype(jnp.bfloat16), ("dp", "expert"), 1),
        *sent_together(
            (
                local_router.astype(jnp.bfloat16),
                local_first_gain.astype(jnp.bfloat16),
                local_first_bias.astype(jnp.bfloat16),
                local_second_gain.astype(jnp.bfloat16),
                local_second_bias.astype(jnp.bfloat16),
            ),
            ("dp", "expert"),
            0,
            1,
        ),
    )
    (
        attention_in_grad,
        attention_out_grad,
        router_grad,
        first_gain_grad,
        first_bias_grad,
        second_gain_grad,
        second_bias_grad,
    ) = summed_shared
    return (
        layer_out,
        input_grad,
        first_gain_grad,
        first_bias_grad,
        attention_in_grad,
        attention_out_grad,
        second_gain_grad,
        second_bias_grad,
        router_grad,
        expert_in_grad,
        expert_out_grad,
    )


def solution(mesh):
    in_specs = (
        P(("dp", "expert"), None),
        P(),
        P(),
        P(None, None, "tensor"),
        P("tensor", None),
        P(),
        P(),
        P(),
        P("expert", None, "tensor"),
        P("expert", "tensor", None),
        P(("dp", "expert"), None),
        P(("dp", "expert"), None),
        P(("dp", "expert"), None),
    )
    out_specs = (
        P(("dp", "expert"), None),
        P(("dp", "expert"), None),
        P(("dp", "expert")),
        P(("dp", "expert")),
        P(None, ("dp", "expert"), "tensor"),
        P("tensor", ("dp", "expert")),
        P(("dp", "expert")),
        P(("dp", "expert")),
        P(("dp", "expert"), None),
        P("expert", "dp", "tensor"),
        P("expert", "tensor", "dp"),
    )
    return jax.shard_map(
        per_device, mesh=mesh, in_specs=in_specs, out_specs=out_specs, check_vma=False
    )
```

profile of v0, /device:TPU:0, one launch (start us, length us, event | category | flops | bytes accessed | tf_op | source)
XLA Modules:
  0.0 338.7 jit_solution(17743377087618630051)
XLA Ops:
  15.5 42.5 %all-reduce.5.cloned.1.call-done = f32[197,768]{1,0:T(8,128)} async-done(((f32[197,768]{1,0:T(8,128)}), f32[197,768]{1,0:T(8,128)}) %all-reduce.5.cloned.1.call-update) | async-done | bytes 605200 | tf_op jit(solution)/shard_map/psum | solution.py:108
  63.6 2.4 copy.130
  66.0 4.2 %all-to-all-start = ((bf16[2,2,98,768]{3,1,2,0:T(2,128)(2,1)}), bf16[2,2,98,768]{3,1,2,0:T(2,128)(2,1)}, u32[]{:S(2)}, u32[]{:S(2)}) async-start(bf16[2,2,98,768]{3,1,2,0:T(2,128)(2,1)} %copy.130), calls=%async_computation | async-start | bytes 1204224 | tf_op jit(solution)/shard_map/all_to_all | solution.py:128
  70.7 2.1 fusion.23
  72.8 2.1 reshape.286
  74.9 2.4 copy.134
  78.8 4.3 %all-to-all-start.2 = ((bf16[2,2,98,768]{3,1,2,0:T(2,128)(2,1)}), bf16[2,2,98,768]{3,1,2,0:T(2,128)(2,1)}, u32[]{:S(2)}, u32[]{:S(2)}) async-start(bf16[2,2,98,768]{3,1,2,0:T(2,128)(2,1)} %copy.134), calls=%async_computation.2 | async-start | bytes 1204224 | tf_op jit(solution)/shard_map/all_to_all | solution.py:156
  83.1 2.5 fusion.14
  89.5 47.3 %all-reduce.10 = bf16[2,2,98,768]{3,1,2,0:T(2,128)(2,1)} all-reduce(f32[2,2,98,768]{3,1,2,0:T(2,128)} %bitcast.163), channel_id=1, replica_groups=mesh['dp'=4,'expert'=2,'tensor'=4] {'tensor'}, use_global_device_ids=true, to_apply=%region_11.12 | all-reduce | flops 301056 | bytes 1806336 | tf_op jit(solution)/shard_map/psum | solution.py:135
  136.7 4.3 %all-to-all-start.1 = ((bf16[2,2,98,768]{3,1,2,0:T(2,128)(2,1)}), bf16[2,2,98,768]{3,1,2,0:T(2,128)(2,1)}, u32[]{:S(2)}, u32[]{:S(2)}) async-start(bf16[2,2,98,768]{3,1,2,0:T(2,128)(2,1)} %all-reduce.10), calls=%async_computation.1 | async-start | bytes 1204224 | tf_op jit(solution)/shard_map/all_to_all | solution.py:136
  141.1 2.9 fusion.17
  150.3 2.1 reshape.301
  152.4 2.8 multiply_reduce_fusion
  155.3 31.0 %all-reduce.7.cloned.1.call-done = bf16[2,2,98,768]{3,2,0,1:T(8,128)(2,1)} async-done(((bf16[2,2,98,768]{3,2,0,1:T(8,128)(2,1)}), bf16[2,2,98,768]{3,2,0,1:T(8,128)(2,1)}) %all-reduce.7.cloned.1.call-update) | async-done | bytes 602128 | tf_op jit(solution)/shard_map/psum | solution.py:172
  186.3 2.4 copy.136
  188.6 4.2 %all-to-all-start.3 = ((bf16[2,2,98,768]{3,1,2,0:T(2,128)(2,1)}), bf16[2,2,98,768]{3,1,2,0:T(2,128)(2,1)}, u32[]{:S(2)}, u32[]{:S(2)}) async-start(bf16[2,2,98,768]{3,1,2,0:T(2,128)(2,1)} %copy.136), calls=%async_computation.3 | async-start | bytes 1204224 | tf_op jit(solution)/shard_map/all_to_all | solution.py:173
  194.7 6.8 %all-to-all-done.3 = bf16[2,2,98,768]{3,1,2,0:T(2,128)(2,1)} async-done(((bf16[2,2,98,768]{3,1,2,0:T(2,128)(2,1)}), bf16[2,2,98,768]{3,1,2,0:T(2,128)(2,1)}, u32[]{:S(2)}, u32[]{:S(2)}) %all-to-all-start.3) | async-done | bytes 602144 | tf_op jit(solution)/shard_map/all_to_all | solution.py:173
  203.5 2.1 reshape.287
  212.7 3.3 bitcast_convert_fusion.1
  216.1 3.8 %bitcast_convert_fusion = bf16[2,768,768]{1,2,0:T(8,128)(2,1)} fusion(bf16[2,2,98,768]{3,1,2,0:T(2,128)(2,1)} %all-to-all-done.2, f32[2,2,98,768]{3,2,0,1:T(8,128)} %copy-done.14), kind=kOutput, calls=%fused_computation | convolution fusion | flops 466311168 | bytes 4165632 | tf_op jit(solution)/shard_map/skcf,skcd->kfd/dot_general | solution.py:163
  222.0 2.2 reshape.295
  226.0 4.1 %all-to-all-start.6 = ((bf16[8,192,96]{2,1,0:T(8,128)(2,1)}), bf16[8,192,96]{2,1,0:T(8,128)(2,1)}, u32[]{:S(2)}, u32[]{:S(2)}) async-start(bf16[8,192,96]{2,1,0:T(8,128)(2,1)} %bitcast.164), calls=%async_computation.6 | async-start | bytes 786432 | tf_op jit(solution)/shard_map/all_to_all | solution.py:21
  231.6 6.3 %all-to-all-done.6 = bf16[8,192,96]{2,1,0:T(8,128)(2,1)} async-done(((bf16[8,192,96]{2,1,0:T(8,128)(2,1)}), bf16[8,192,96]{2,1,0:T(8,128)(2,1)}, u32[]{:S(2)}, u32[]{:S(2)}) %all-to-all-start.6) | async-done | bytes 294944 | tf_op jit(solution)/shard_map/all_to_all | solution.py:21
  239.5 8.2 %all-reduce.9.cloned.1.call-done = bf16[197,768]{1,0:T(8,128)(2,1)} async-done(((bf16[197,768]{1,0:T(8,128)(2,1)}), bf16[197,768]{1,0:T(8,128)(2,1)}) %all-reduce.9.cloned.1.call-update) | async-done | bytes 302608 | tf_op jit(solution)/shard_map/psum | solution.py:238
  251.6 3.6 %all-to-all-start.4 = ((bf16[8,96,8]{1,2,0:T(8,128)(2,1)}), bf16[8,96,8]{1,2,0:T(8,128)(2,1)S(1)}, u32[]{:S(2)}, u32[]{:S(2)}) async-start(bf16[8,96,8]{1,2,0:T(8,128)(2,1)} %concatenate.12), calls=%async_computation.4 | async-start | bytes 32768 | tf_op jit(solution)/shard_map/all_to_all | solution.py:21
  261.5 4.3 %all-to-all-start.5 = ((bf16[8,3,96,192]{3,2,1,0:T(8,128)(2,1)}), bf16[8,3,96,192]{3,2,1,0:T(8,128)(2,1)}, u32[]{:S(2)}, u32[]{:S(2)}) async-start(bf16[8,3,96,192]{3,2,1,0:T(8,128)(2,1)} %copy.150), calls=%async_computation.5 | async-start | bytes 2359296 | tf_op jit(solution)/shard_map/all_to_all | solution.py:21
  269.0 19.1 %all-to-all-done.5 = bf16[8,3,96,192]{3,2,1,0:T(8,128)(2,1)} async-done(((bf16[8,3,96,192]{3,2,1,0:T(8,128)(2,1)}), bf16[8,3,96,192]{3,2,1,0:T(8,128)(2,1)}, u32[]{:S(2)}, u32[]{:S(2)}) %all-to-all-start.5) | async-done | bytes 884768 | tf_op jit(solution)/shard_map/all_to_all | solution.py:21
  288.0 2.2 convert_reduce_fusion
  290.2 5.2 %reduce-scatter.3.cloned.1.call-done = bf16[2,192,768]{2,1,0:T(8,128)(2,1)} async-done(((bf16[2,768,768]{2,1,0:T(8,128)(2,1)}), bf16[2,192,768]{2,1,0:T(8,128)(2,1)}) %reduce-scatter.3.cloned.1.call-update) | async-done | bytes 589840 | tf_op jit(solution)/shard_map/reduce_scatter | solution.py:181
  295.4 2.2 convert_element_type.252
  297.6 32.4 %reduce-scatter.5.cloned.1.call-done = bf16[2,768,192]{1,2,0:T(8,128)(2,1)} async-done(((bf16[2,768,768]{1,2,0:T(8,128)(2,1)}), bf16[2,768,192]{1,2,0:T(8,128)(2,1)}) %reduce-scatter.5.cloned.1.call-update) | async-done | bytes 589840 | tf_op jit(solution)/shard_map/reduce_scatter | solution.py:184
  330.0 2.2 convert_element_type.254
  (170 shorter events, 57.0 us)
Async XLA Ops:
  7.2 79.5 %copy-start = (bf16[2,768,768]{2,1,0:T(8,128)(2,1)S(1)}, bf16[2,768,768]{2,1,0:T(8,128)(2,1)}, u32[]{:S(2)}) copy-start(bf16[2,768,768]{2,1,0:T(8,128)(2,1)} %param.22) | copy-start | bytes 7077892
  7.2 4.1 %copy-start.6 = (bf16[197,768]{1,0:T(8,128)(2,1)S(1)}, bf16[197,768]{1,0:T(8,128)(2,1)}, u32[]{:S(2)}) copy-start(bf16[197,768]{1,0:T(8,128)(2,1)} %param.13) | copy-start | bytes 907780
  7.2 4.1 %copy-start.17 = (bf16[3,768,192]{1,2,0:T(8,128)(2,1)S(1)}, bf16[3,768,192]{1,2,0:T(8,128)(2,1)}, u32[]{:S(2)}) copy-start(bf16[3,768,192]{1,2,0:T(8,128)(2,1)} %param.16) | copy-start | bytes 2654212
  7.2 50.8 %all-reduce.5.cloned.1.call-start = ((), (), s32[]{:S(2)}) async-start(), calls=%async_computation.9 | async-start | bytes 1228800 | tf_op jit(solution)/shard_map/psum | solution.py:108
  7.3 4.0 %copy-start.34 = (f32[768]{0:T(1024)S(1)}, f32[768]{0:T(1024)}, u32[]{:S(2)}) copy-start(f32[768]{0:T(1024)} %param.14) | copy-start | bytes 9220
  7.3 4.0 %copy-start.39 = (f32[768]{0:T(1024)S(1)}, f32[768]{0:T(1024)}, u32[]{:S(2)}) copy-start(f32[768]{0:T(1024)} %param.15) | copy-start | bytes 9220
  12.1 2.1 copy-start.15
  12.6 2.7 copy-start.32
  12.6 2.7 copy-start.33
  15.3 44.1 %copy-start.31 = (f32[768]{0:T(1024)S(1)}, f32[768]{0:T(1024)}, u32[]{:S(2)}) copy-start(f32[768]{0:T(1024)} %param.18) | copy-start | bytes 9220
  15.3 44.1 %copy-start.38 = (f32[768]{0:T(1024)S(1)}, f32[768]{0:T(1024)}, u32[]{:S(2)}) copy-start(f32[768]{0:T(1024)} %param.19) | copy-start | bytes 9220
  15.5 44.2 %copy-start.30 = (f32[768,4]{0,1:T(4,128)S(1)}, f32[768,4]{0,1:T(4,128)}, u32[]{:S(2)}) copy-start(f32[768,4]{0,1:T(4,128)} %param.20) | copy-start | bytes 36868
  66.0 12.8 %all-to-all-start = ((bf16[2,2,98,768]{3,1,2,0:T(2,128)(2,1)}), bf16[2,2,98,768]{3,1,2,0:T(2,128)(2,1)}, u32[]{:S(2)}, u32[]{:S(2)}) async-start(bf16[2,2,98,768]{3,1,2,0:T(2,128)(2,1)} %copy.130), calls=%async_computation | async-start | bytes 1204224 | tf_op jit(solution)/shard_map/all_to_all | solution.py:128
  78.8 58.0 %all-to-all-start.2 = ((bf16[2,2,98,768]{3,1,2,0:T(2,128)(2,1)}), bf16[2,2,98,768]{3,1,2,0:T(2,128)(2,1)}, u32[]{:S(2)}, u32[]{:S(2)}) async-start(bf16[2,2,98,768]{3,1,2,0:T(2,128)(2,1)} %copy.134), calls=%async_computation.2 | async-start | bytes 1204224 | tf_op jit(solution)/shard_map/all_to_all | solution.py:156
  136.7 11.6 %all-to-all-start.1 = ((bf16[2,2,98,768]{3,1,2,0:T(2,128)(2,1)}), bf16[2,2,98,768]{3,1,2,0:T(2,128)(2,1)}, u32[]{:S(2)}, u32[]{:S(2)}) async-start(bf16[2,2,98,768]{3,1,2,0:T(2,128)(2,1)} %all-reduce.10), calls=%async_computation.1 | async-start | bytes 1204224 | tf_op jit(solution)/shard_map/all_to_all | solution.py:136
  141.0 45.3 %all-reduce.7.cloned.1.call-start = ((), (), s32[]{:S(2)}) async-start(), calls=%async_computation.10 | async-start | bytes 1277952 | tf_op jit(solution)/shard_map/psum | solution.py:172
  141.1 3.7 %copy-start.5 = (bf16[2,768,768]{2,1,0:T(8,128)(2,1)S(1)}, bf16[2,768,768]{2,1,0:T(8,128)(2,1)}, u32[]{:S(2)}) copy-start(bf16[2,768,768]{2,1,0:T(8,128)(2,1)} %param.21) | copy-start | bytes 7077892
  188.6 12.9 %all-to-all-start.3 = ((bf16[2,2,98,768]{3,1,2,0:T(2,128)(2,1)}), bf16[2,2,98,768]{3,1,2,0:T(2,128)(2,1)}, u32[]{:S(2)}, u32[]{:S(2)}) async-start(bf16[2,2,98,768]{3,1,2,0:T(2,128)(2,1)} %copy.136), calls=%async_computation.3 | async-start | bytes 1204224 | tf_op jit(solution)/shard_map/all_to_all | solution.py:173
  192.9 54.9 %all-reduce.9.cloned.1.call-start = ((), (), s32[]{:S(2)}) async-start(), calls=%async_computation.11 | async-start | bytes 614400 | tf_op jit(solution)/shard_map/psum | solution.py:238
  205.6 2.0 copy-start.9
  205.6 2.0 copy-start.23
  212.7 82.8 %reduce-scatter.3.cloned.1.call-start = ((), (), s32[]{:S(2)}) async-start(), calls=%async_computation.12 | async-start | bytes 2949120 | tf_op jit(solution)/shard_map/reduce_scatter | solution.py:181
  216.1 113.9 %reduce-scatter.5.cloned.1.call-start = ((), (), s32[]{:S(2)}) async-start(), calls=%async_computation.13 | async-start | bytes 2949120 | tf_op jit(solution)/shard_map/reduce_scatter | solution.py:184
  224.1 23.6 %copy-start.35 = (f32[768]{0:T(1024)S(1)}, f32[768]{0:T(1024)}, u32[]{:S(2)}) copy-start(f32[768]{0:T(1024)} %param.14) | copy-start | bytes 9220
  224.1 23.6 %copy-start.37 = (f32[197]{0:T(256)S(1)}, f32[197]{0:T(256)}, u32[]{:S(2)}) copy-start(f32[197]{0:T(256)} %copy-done.36) | copy-start | bytes 2368
  224.1 23.6 %copy-start.40 = (f32[768]{0:T(1024)S(1)}, f32[768]{0:T(1024)}, u32[]{:S(2)}) copy-start(f32[768]{0:T(1024)} %param.15) | copy-start | bytes 9220
  226.0 11.9 %all-to-all-start.6 = ((bf16[8,192,96]{2,1,0:T(8,128)(2,1)}), bf16[8,192,96]{2,1,0:T(8,128)(2,1)}, u32[]{:S(2)}, u32[]{:S(2)}) async-start(bf16[8,192,96]{2,1,0:T(8,128)(2,1)} %bitcast.164), calls=%async_computation.6 | async-start | bytes 786432 | tf_op jit(solution)/shard_map/all_to_all | solution.py:21
  239.5 18.9 %copy-start.20 = (bf16[3,64,197]{2,1,0:T(8,128)(2,1)S(1)}, bf16[3,64,197]{2,1,0:T(8,128)(2,1)}, u32[]{:S(2)}) copy-start(bf16[3,64,197]{2,1,0:T(8,128)(2,1)} %copy-done.19) | copy-start | bytes 226948
  251.6 9.9 %all-to-all-start.4 = ((bf16[8,96,8]{1,2,0:T(8,128)(2,1)}), bf16[8,96,8]{1,2,0:T(8,128)(2,1)S(1)}, u32[]{:S(2)}, u32[]{:S(2)}) async-start(bf16[8,96,8]{1,2,0:T(8,128)(2,1)} %concatenate.12), calls=%async_computation.4 | async-start | bytes 32768 | tf_op jit(solution)/shard_map/all_to_all | solution.py:21
  257.1 2.7 copy-start.7
  257.1 2.7 copy-start.22
  261.5 26.5 %all-to-all-start.5 = ((bf16[8,3,96,192]{3,2,1,0:T(8,128)(2,1)}), bf16[8,3,96,192]{3,2,1,0:T(8,128)(2,1)}, u32[]{:S(2)}, u32[]{:S(2)}) async-start(bf16[8,3,96,192]{3,2,1,0:T(8,128)(2,1)} %copy.150), calls=%async_computation.5 | async-start | bytes 2359296 | tf_op jit(solution)/shard_map/all_to_all | solution.py:21
  (21 other events, 25.8 us)
Sparse Core Ops, SparseCore 0:
  15.4 42.5 all-reduce.4
  146.6 39.5 all-reduce.6
  212.8 34.9 all-reduce.8
  250.1 45.2 reduce-scatter.2
  297.8 32.1 reduce-scatter.4
where the time goes:
time: 341 us; the launch traced here: 339 us
  waiting for transfers between devices  153 us (45%)
  blocking collectives  47.3 us (14%)
  matrix products  37.3 us (11%)
  local copies, waits for them, and re-layouts  36.2 us (11%)
  starting transfers between devices  29.3 us (9%)
  other arithmetic  21 us (6%)
  between operations  14.5 us (4%)
    psum x1, blocking collectives, per_device(): summed = lax.psum(partial_value, 'tensor')  47.3 us
    psum x1, waiting for transfers between devices, per_device(): attended = lax.psum(partial_attn, 'tensor')  42.5 us
    reduce_scatter x1, waiting for transfers between devices, per_device(): lax.psum_scatter(local_out_grad.astype(jnp.bfloat16), 'dp', scatter_dimen...  32.4 us
    psum x1, waiting for transfers between devices, per_device(): back_sum = lax.psum(partial_back.astype(jnp.bfloat16), 'tensor')  31 us
    all_to_all x3, waiting for transfers between devices, sent_and_summed(): lax.all_to_all(cut_along(shard, dim, devices), axis, 0, 0, tiled=True)  25.3 us
    all_to_all x3, starting transfers between devices, sent_and_summed(): lax.all_to_all(cut_along(shard, dim, devices), axis, 0, 0, tiled=True)  11.9 us
    psum x1, waiting for transfers between devices, per_device(): lax.psum(partial_first.astype(jnp.bfloat16), 'tensor').astype(jnp.float32)  8.2 us
    all_to_all x1, waiting for transfers between devices, per_device(): lax.all_to_all(back_sum, 'expert', split_axis=0, concat_axis=0, tiled=True)  6.82 us
  transfers between devices with their start and end apart: 12, of which 9 were waited for; matrix products, arithmetic and copies ran while one was open for 18% of the time, Pallas kernels for 0%

commit v1 on v0

--- a/solution.py
+++ b/solution.py
@@ -3,6 +3,7 @@
 import jax.numpy as jnp
 from jax import lax
 from jax.sharding import PartitionSpec as P
+from jax.lax import axis_size, ppermute
 
 HEAD_DIM = 64
 SEQ = 197
@@ -132,7 +133,12 @@
     partial_value = jnp.einsum(
         "skcf,kfd->skcd", hidden, expert_out, preferred_element_type=jnp.float32
     )
-    summed = lax.psum(partial_value, "tensor")
+    cores_n = axis_size("tensor")
+    summed = partial_value
+    for at in [kk for kk in (1, 2, 4, 8, 16) if kk < cores_n]:
+        summed = summed + ppermute(
+            summed, axis_name="tensor", perm=[(d, d ^ at) for d in range(cores_n)]
+        )
     returned = lax.all_to_all(
         summed.astype(jnp.bfloat16), "expert", split_axis=0, concat_axis=0, tiled=True
     )

time: 341 us -> 356 us (1.044)
  waiting for transfers between devices: 153 us -> 204 us
  blocking collectives: 47.3 us -> 10.9 us
  matrix products: 37.3 us -> 31.6 us
  local copies, waits for them, and re-layouts: 36.2 us -> 41.7 us
  other arithmetic: 21 us -> 24.6 us
    psum x1 -> x0, blocking collectives: 47.3 us -> none  [per_device(): summed = lax.psum(partial_value, 'tensor')]
    psum x1, waiting for transfers between devices: 31 us -> 60.9 us  [per_device(): back_sum = lax.psum(partial_back.astype(jnp.bfloat16), 'tensor')]
    ppermute x0 -> x2, waiting for transfers between devices: none -> 15.6 us  [per_device(): ppermute(summed, axis_name='tensor', perm=[(d, d ^ at) for d in range(cor...]
    all_to_all x0 -> x1, blocking collectives: none -> 10.9 us  [per_device(): lax.all_to_all(sendbuf, 'expert', split_axis=0, concat_axis=0, tiled=True)]
    psum x1, waiting for transfers between devices: 8.2 us -> 13.8 us  [per_device(): lax.psum(partial_first.astype(jnp.bfloat16), 'tensor').astype(jnp.float32)]
    all_to_all x1 -> x0, starting transfers between devices: 4.24 us -> none  [per_device(): lax.all_to_all(sendbuf, 'expert', split_axis=0, concat_axis=0, tiled=True)]
    unnamed x82 -> x92, local copies, waits for them, and re-layouts: 5.77 us -> 8.67 us
  transfers between devices with their start and end apart: 12 -> 13, of which waited for: 9 -> 11; matrix products, arithmetic and copies ran while one was open for 18% -> 17% of each run, Pallas kernels for 0% -> 0%
where the time goes in v1:
time: 356 us; the launch traced here: 354 us
  waiting for transfers between devices  204 us (57%)
  local copies, waits for them, and re-layouts  41.7 us (12%)
  matrix products  31.6 us (9%)
  starting transfers between devices  26.7 us (8%)
  other arithmetic  24.6 us (7%)
  between operations  14.5 us (4%)
  blocking collectives  10.9 us (3%)
    psum x1, waiting for transfers between devices, per_device(): back_sum = lax.psum(partial_back.astype(jnp.bfloat16), 'tensor')  60.9 us
    psum x1, waiting for transfers between devices, per_device(): attended = lax.psum(partial_attn, 'tensor')  42.5 us
    reduce_scatter x1, waiting for transfers between devices, per_device(): lax.psum_scatter(local_out_grad.astype(jnp.bfloat16), 'dp', scatter_dimen...  32.4 us
    all_to_all x3, waiting for transfers between devices, sent_and_summed(): lax.all_to_all(cut_along(shard, dim, devices), axis, 0, 0, tiled=True)  25.7 us
    ppermute x2, waiting for transfers between devices, per_device(): ppermute(summed, axis_name='tensor', perm=[(d, d ^ at) for d in range(cor...  15.6 us
    psum x1, waiting for transfers between devices, per_device(): lax.psum(partial_first.astype(jnp.bfloat16), 'tensor').astype(jnp.float32)  13.8 us
    all_to_all x3, starting transfers between devices, sent_and_summed(): lax.all_to_all(cut_along(shard, dim, devices), axis, 0, 0, tiled=True)  11.9 us
    all_to_all x1, blocking collectives, per_device(): lax.all_to_all(sendbuf, 'expert', split_axis=0, concat_axis=0, tiled=True)  10.9 us
  transfers between devices with their start and end apart: 13, of which 11 were waited for; matrix products, arithmetic and copies ran while one was open for 17% of the time, Pallas kernels for 0%

profile of v1, /device:TPU:0, one launch (start us, length us, event | category | flops | bytes accessed | tf_op | source)
XLA Modules:
  0.0 354.0 jit_solution(6454791159591241539)
XLA Ops:
  15.5 42.5 %all-reduce.4.cloned.1.call-done = f32[197,768]{1,0:T(8,128)} async-done(((f32[197,768]{1,0:T(8,128)}), f32[197,768]{1,0:T(8,128)}) %all-reduce.4.cloned.1.call-update) | async-done | bytes 605200 | tf_op jit(solution)/shard_map/psum | solution.py:109
  61.5 2.1 reshape.284
  65.2 10.9 %all_to_all.35 = bf16[2,2,98,768]{3,1,2,0:T(2,128)(2,1)S(1)} all-to-all(bf16[2,2,98,768]{3,1,2,0:T(2,128)(2,1)S(1)} %copy.113), channel_id=1, replica_groups=mesh['dp'=4,'expert'=2,'tensor'=4] {'expert'}, dimensions={0} | all-to-all | bytes 1204224 | tf_op jit(solution)/shard_map/all_to_all | solution.py:129
  84.2 2.1 reshape.286
  86.3 2.4 copy.121
  88.7 4.2 %all-to-all-start.2 = ((bf16[2,2,98,768]{3,1,2,0:T(2,128)(2,1)}), bf16[2,2,98,768]{3,1,2,0:T(2,128)(2,1)}, u32[]{:S(2)}, u32[]{:S(2)}) async-start(bf16[2,2,98,768]{3,1,2,0:T(2,128)(2,1)} %copy.121), calls=%async_computation.2 | async-start | bytes 1204224 | tf_op jit(solution)/shard_map/all_to_all | solution.py:162
  92.9 15.6 %collective-permute-done = f32[2,2,98,768]{3,1,2,0:T(2,128)} collective-permute-done((f32[2,2,98,768]{3,1,2,0:T(2,128)}, f32[2,2,98,768]{3,1,2,0:T(2,128)}, u32[]{:S(2)}, u32[]{:S(2)}) %collective-permute-start) | collective-permute-done | bytes 1204256 | tf_op jit(solution)/shard_map/ppermute | solution.py:139
  114.5 2.9 fusion.20
  120.0 60.9 %all-reduce.6.cloned.1.call-done = bf16[2,2,98,768]{3,2,0,1:T(8,128)(2,1)} async-done(((bf16[2,2,98,768]{3,2,0,1:T(8,128)(2,1)}), bf16[2,2,98,768]{3,2,0,1:T(8,128)(2,1)}) %all-reduce.6.cloned.1.call-update) | async-done | bytes 602128 | tf_op jit(solution)/shard_map/psum | solution.py:178
  180.9 2.4 copy.123
  183.2 4.2 %all-to-all-start.3 = ((bf16[2,2,98,768]{3,1,2,0:T(2,128)(2,1)}), bf16[2,2,98,768]{3,1,2,0:T(2,128)(2,1)}, u32[]{:S(2)}, u32[]{:S(2)}) async-start(bf16[2,2,98,768]{3,1,2,0:T(2,128)(2,1)} %copy.123), calls=%async_computation.3 | async-start | bytes 1204224 | tf_op jit(solution)/shard_map/all_to_all | solution.py:179
  190.6 5.8 %all-to-all-done.3 = bf16[2,2,98,768]{3,1,2,0:T(2,128)(2,1)} async-done(((bf16[2,2,98,768]{3,1,2,0:T(2,128)(2,1)}), bf16[2,2,98,768]{3,1,2,0:T(2,128)(2,1)}, u32[]{:S(2)}, u32[]{:S(2)}) %all-to-all-start.3) | async-done | bytes 602144 | tf_op jit(solution)/shard_map/all_to_all | solution.py:179
  196.4 4.4 %all-to-all-start.1 = ((bf16[2,2,98,768]{3,1,2,0:T(2,128)(2,1)}), bf16[2,2,98,768]{3,1,2,0:T(2,128)(2,1)}, u32[]{:S(2)}, u32[]{:S(2)}) async-start(bf16[2,2,98,768]{3,1,2,0:T(2,128)(2,1)} %copy.119), calls=%async_computation.1 | async-start | bytes 1204224 | tf_op jit(solution)/shard_map/all_to_all | solution.py:142
  204.7 2.1 reshape.287
  206.8 2.2 all-to-all-done.1
  210.9 2.1 reshape.301
  213.0 2.1 multiply_reduce_fusion
  222.3 3.3 bitcast_convert_fusion.1
  225.6 3.8 %bitcast_convert_fusion = bf16[2,768,768]{1,2,0:T(8,128)(2,1)} fusion(bf16[2,2,98,768]{3,1,2,0:T(2,128)(2,1)} %all-to-all-done.2, f32[2,2,98,768]{3,2,0,1:T(8,128)} %copy-done.21), kind=kOutput, calls=%fused_computation | convolution fusion | flops 466311168 | bytes 4165632 | tf_op jit(solution)/shard_map/skcf,skcd->kfd/dot_general | solution.py:169
  231.5 2.2 reshape.295
  235.5 4.1 %all-to-all-start.6 = ((bf16[8,192,96]{2,1,0:T(8,128)(2,1)}), bf16[8,192,96]{2,1,0:T(8,128)(2,1)}, u32[]{:S(2)}, u32[]{:S(2)}) async-start(bf16[8,192,96]{2,1,0:T(8,128)(2,1)} %bitcast.164), calls=%async_computation.6 | async-start | bytes 786432 | tf_op jit(solution)/shard_map/all_to_all | solution.py:22
  241.1 6.3 %all-to-all-done.6 = bf16[8,192,96]{2,1,0:T(8,128)(2,1)} async-done(((bf16[8,192,96]{2,1,0:T(8,128)(2,1)}), bf16[8,192,96]{2,1,0:T(8,128)(2,1)}, u32[]{:S(2)}, u32[]{:S(2)}) %all-to-all-start.6) | async-done | bytes 294944 | tf_op jit(solution)/shard_map/all_to_all | solution.py:22
  249.1 13.8 %all-reduce.8.cloned.1.call-done = bf16[197,768]{1,0:T(8,128)(2,1)} async-done(((bf16[197,768]{1,0:T(8,128)(2,1)}), bf16[197,768]{1,0:T(8,128)(2,1)}) %all-reduce.8.cloned.1.call-update) | async-done | bytes 302608 | tf_op jit(solution)/shard_map/psum | solution.py:244
  268.6 3.6 %all-to-all-start.4 = ((bf16[8,96,8]{1,2,0:T(8,128)(2,1)}), bf16[8,96,8]{1,2,0:T(8,128)(2,1)S(1)}, u32[]{:S(2)}, u32[]{:S(2)}) async-start(bf16[8,96,8]{1,2,0:T(8,128)(2,1)} %concatenate.12), calls=%async_computation.4 | async-start | bytes 32768 | tf_op jit(solution)/shard_map/all_to_all | solution.py:22
  276.9 4.3 %all-to-all-start.5 = ((bf16[8,3,96,192]{3,2,1,0:T(8,128)(2,1)}), bf16[8,3,96,192]{3,2,1,0:T(8,128)(2,1)}, u32[]{:S(2)}, u32[]{:S(2)}) async-start(bf16[8,3,96,192]{3,2,1,0:T(8,128)(2,1)} %copy.137), calls=%async_computation.5 | async-start | bytes 2359296 | tf_op jit(solution)/shard_map/all_to_all | solution.py:22
  281.1 2.1 fusion.57
  284.3 19.1 %all-to-all-done.5 = bf16[8,3,96,192]{3,2,1,0:T(8,128)(2,1)} async-done(((bf16[8,3,96,192]{3,2,1,0:T(8,128)(2,1)}), bf16[8,3,96,192]{3,2,1,0:T(8,128)(2,1)}, u32[]{:S(2)}, u32[]{:S(2)}) %all-to-all-start.5) | async-done | bytes 884768 | tf_op jit(solution)/shard_map/all_to_all | solution.py:22
  303.4 2.2 convert_reduce_fusion
  305.6 5.1 %reduce-scatter.3.cloned.1.call-done = bf16[2,192,768]{2,1,0:T(8,128)(2,1)} async-done(((bf16[2,768,768]{2,1,0:T(8,128)(2,1)}), bf16[2,192,768]{2,1,0:T(8,128)(2,1)}) %reduce-scatter.3.cloned.1.call-update) | async-done | bytes 589840 | tf_op jit(solution)/shard_map/reduce_scatter | solution.py:187
  310.8 2.2 convert_element_type.252
  312.9 32.4 %reduce-scatter.5.cloned.1.call-done = bf16[2,768,192]{1,2,0:T(8,128)(2,1)} async-done(((bf16[2,768,768]{1,2,0:T(8,128)(2,1)}), bf16[2,768,192]{1,2,0:T(8,128)(2,1)}) %reduce-scatter.5.cloned.1.call-update) | async-done | bytes 589840 | tf_op jit(solution)/shard_map/reduce_scatter | solution.py:190
  345.3 2.2 convert_element_type.254
  (186 shorter events, 64.4 us)
Async XLA Ops:
  7.2 71.5 %copy-start = (bf16[2,768,768]{2,1,0:T(8,128)(2,1)S(1)}, bf16[2,768,768]{2,1,0:T(8,128)(2,1)}, u32[]{:S(2)}) copy-start(bf16[2,768,768]{2,1,0:T(8,128)(2,1)} %param.22) | copy-start | bytes 7077892
  7.2 4.1 %copy-start.8 = (bf16[197,768]{1,0:T(8,128)(2,1)S(1)}, bf16[197,768]{1,0:T(8,128)(2,1)}, u32[]{:S(2)}) copy-start(bf16[197,768]{1,0:T(8,128)(2,1)} %param.13) | copy-start | bytes 907780
  7.2 4.1 %copy-start.24 = (bf16[3,768,192]{1,2,0:T(8,128)(2,1)S(1)}, bf16[3,768,192]{1,2,0:T(8,128)(2,1)}, u32[]{:S(2)}) copy-start(bf16[3,768,192]{1,2,0:T(8,128)(2,1)} %param.16) | copy-start | bytes 2654212
  7.2 50.8 %all-reduce.4.cloned.1.call-start = ((), (), s32[]{:S(2)}) async-start(), calls=%async_computation.9 | async-start | bytes 1228800 | tf_op jit(solution)/shard_map/psum | solution.py:109
  7.3 4.0 %copy-start.39 = (f32[768]{0:T(1024)S(1)}, f32[768]{0:T(1024)}, u32[]{:S(2)}) copy-start(f32[768]{0:T(1024)} %param.14) | copy-start | bytes 9220
  7.3 4.0 %copy-start.44 = (f32[768]{0:T(1024)S(1)}, f32[768]{0:T(1024)}, u32[]{:S(2)}) copy-start(f32[768]{0:T(1024)} %param.15) | copy-start | bytes 9220
  12.6 2.7 copy-start.37
  12.6 2.7 copy-start.38
  15.3 44.1 %copy-start.36 = (f32[768]{0:T(1024)S(1)}, f32[768]{0:T(1024)}, u32[]{:S(2)}) copy-start(f32[768]{0:T(1024)} %param.18) | copy-start | bytes 9220
  15.3 44.1 %copy-start.43 = (f32[768]{0:T(1024)S(1)}, f32[768]{0:T(1024)}, u32[]{:S(2)}) copy-start(f32[768]{0:T(1024)} %param.19) | copy-start | bytes 9220
  63.5 13.4 %copy-start.6 = (bf16[2,768,768]{2,1,0:T(8,128)(2,1)S(1)}, bf16[2,768,768]{2,1,0:T(8,128)(2,1)}, u32[]{:S(2)}) copy-start(bf16[2,768,768]{2,1,0:T(8,128)(2,1)} %param.21) | copy-start | bytes 7077892
  79.5 3.0 copy-start.12
  79.6 3.5 copy-start.15
  81.6 26.9 %collective-permute-start = (f32[2,2,98,768]{3,1,2,0:T(2,128)}, f32[2,2,98,768]{3,1,2,0:T(2,128)}, u32[]{:S(2)}, u32[]{:S(2)}) collective-permute-start(f32[2,2,98,768]{3,1,2,0:T(2,128)} %copy.115), channel_id=1, source_target_pairs={{0,1},{1,0},{2,3},{3,2},{4,5},{5,4},{6,7},{7,6},{8,9},{9,8},{10,11... | collective-permute-start | bytes 3612680 | tf_op jit(solution)/shard_map/ppermute | solution.py:139
  88.7 25.9 %all-to-all-start.2 = ((bf16[2,2,98,768]{3,1,2,0:T(2,128)(2,1)}), bf16[2,2,98,768]{3,1,2,0:T(2,128)(2,1)}, u32[]{:S(2)}, u32[]{:S(2)}) async-start(bf16[2,2,98,768]{3,1,2,0:T(2,128)(2,1)} %copy.121), calls=%async_computation.2 | async-start | bytes 1204224 | tf_op jit(solution)/shard_map/all_to_all | solution.py:162
  92.9 88.0 %all-reduce.6.cloned.1.call-start = ((), (), s32[]{:S(2)}) async-start(), calls=%async_computation.10 | async-start | bytes 1277952 | tf_op jit(solution)/shard_map/psum | solution.py:178
  113.4 74.1 %collective-permute-start.1 = (f32[2,2,98,768]{3,1,2,0:T(2,128)}, f32[2,2,98,768]{3,1,2,0:T(2,128)}, u32[]{:S(2)}, u32[]{:S(2)}) collective-permute-start(f32[2,2,98,768]{3,1,2,0:T(2,128)} %copy.117), channel_id=1, source_target_pairs={{0,2},{1,3},{2,0},{3,1},{4,6},{5,7},{6,4},{7,5},{8,10},{9,11},{10,... | collective-permute-start | bytes 3612680 | tf_op jit(solution)/shard_map/ppermute | solution.py:139
  114.5 3.7 %copy-start.7 = (bf16[2,768,768]{2,1,0:T(8,128)(2,1)S(1)}, bf16[2,768,768]{2,1,0:T(8,128)(2,1)}, u32[]{:S(2)}) copy-start(bf16[2,768,768]{2,1,0:T(8,128)(2,1)} %param.21) | copy-start | bytes 7077892
  183.2 13.2 %all-to-all-start.3 = ((bf16[2,2,98,768]{3,1,2,0:T(2,128)(2,1)}), bf16[2,2,98,768]{3,1,2,0:T(2,128)(2,1)}, u32[]{:S(2)}, u32[]{:S(2)}) async-start(bf16[2,2,98,768]{3,1,2,0:T(2,128)(2,1)} %copy.123), calls=%async_computation.3 | async-start | bytes 1204224 | tf_op jit(solution)/shard_map/all_to_all | solution.py:179
  196.4 12.5 %all-to-all-start.1 = ((bf16[2,2,98,768]{3,1,2,0:T(2,128)(2,1)}), bf16[2,2,98,768]{3,1,2,0:T(2,128)(2,1)}, u32[]{:S(2)}, u32[]{:S(2)}) async-start(bf16[2,2,98,768]{3,1,2,0:T(2,128)(2,1)} %copy.119), calls=%async_computation.1 | async-start | bytes 1204224 | tf_op jit(solution)/shard_map/all_to_all | solution.py:142
  200.8 62.0 %all-reduce.8.cloned.1.call-start = ((), (), s32[]{:S(2)}) async-start(), calls=%async_computation.11 | async-start | bytes 614400 | tf_op jit(solution)/shard_map/psum | solution.py:244
  212.9 2.9 copy-start.18
  222.2 88.6 %reduce-scatter.3.cloned.1.call-start = ((), (), s32[]{:S(2)}) async-start(), calls=%async_computation.12 | async-start | bytes 2949120 | tf_op jit(solution)/shard_map/reduce_scatter | solution.py:187
  225.6 119.7 %reduce-scatter.5.cloned.1.call-start = ((), (), s32[]{:S(2)}) async-start(), calls=%async_computation.13 | async-start | bytes 2949120 | tf_op jit(solution)/shard_map/reduce_scatter | solution.py:190
  233.6 29.2 %copy-start.40 = (f32[768]{0:T(1024)S(1)}, f32[768]{0:T(1024)}, u32[]{:S(2)}) copy-start(f32[768]{0:T(1024)} %param.14) | copy-start | bytes 9220
  233.6 29.2 %copy-start.42 = (f32[197]{0:T(256)S(1)}, f32[197]{0:T(256)}, u32[]{:S(2)}) copy-start(f32[197]{0:T(256)} %copy-done.41) | copy-start | bytes 2368
  233.6 29.2 %copy-start.45 = (f32[768]{0:T(1024)S(1)}, f32[768]{0:T(1024)}, u32[]{:S(2)}) copy-start(f32[768]{0:T(1024)} %param.15) | copy-start | bytes 9220
  235.5 11.9 %all-to-all-start.6 = ((bf16[8,192,96]{2,1,0:T(8,128)(2,1)}), bf16[8,192,96]{2,1,0:T(8,128)(2,1)}, u32[]{:S(2)}, u32[]{:S(2)}) async-start(bf16[8,192,96]{2,1,0:T(8,128)(2,1)} %bitcast.164), calls=%async_computation.6 | async-start | bytes 786432 | tf_op jit(solution)/shard_map/all_to_all | solution.py:22
  249.1 24.5 %copy-start.27 = (bf16[3,64,197]{2,1,0:T(8,128)(2,1)S(1)}, bf16[3,64,197]{2,1,0:T(8,128)(2,1)}, u32[]{:S(2)}) copy-start(bf16[3,64,197]{2,1,0:T(8,128)(2,1)} %copy-done.26) | copy-start | bytes 226948
  268.6 8.3 %all-to-all-start.4 = ((bf16[8,96,8]{1,2,0:T(8,128)(2,1)}), bf16[8,96,8]{1,2,0:T(8,128)(2,1)S(1)}, u32[]{:S(2)}, u32[]{:S(2)}) async-start(bf16[8,96,8]{1,2,0:T(8,128)(2,1)} %concatenate.12), calls=%async_computation.4 | async-start | bytes 32768 | tf_op jit(solution)/shard_map/all_to_all | solution.py:22
  272.2 2.7 copy-start.9
  276.9 26.5 %all-to-all-start.5 = ((bf16[8,3,96,192]{3,2,1,0:T(8,128)(2,1)}), bf16[8,3,96,192]{3,2,1,0:T(8,128)(2,1)}, u32[]{:S(2)}, u32[]{:S(2)}) async-start(bf16[8,3,96,192]{3,2,1,0:T(8,128)(2,1)} %copy.137), calls=%async_computation.5 | async-start | bytes 2359296 | tf_op jit(solution)/shard_map/all_to_all | solution.py:22
  (27 other events, 34.6 us)
Sparse Core Ops, SparseCore 0:
  15.4 42.5 all-reduce.3
  120.1 60.7 all-reduce.5
  222.3 40.4 all-reduce.7
  265.2 45.4 reduce-scatter.2
  313.2 32.1 reduce-scatter.4
